TPU v7x, 32 devices: a whole 2x2x4 slice. The times are simulated.
32 devices in a mesh: edge: 4 (over y, x), tile: 8 (over z, core).
Axes of the slice: x: 2, y: 2, z: 4, core: 2. Of those that a mesh axis runs over, the one named last changes fastest.
Arguments:
- features: bfloat16 [96, 48, 64, 128], P('edge', 'tile'), may hold values from -6 to 6
- hidden_state: bfloat16 [32, 48, 64, 128], P('edge', 'tile'), may hold values from -1 to 1
- edge_source: int32 [32], P('edge'), may hold values from 0 to 23
- edge_owner: int32 [32, 1], P('edge'), may hold values from 0 to 3; in each aligned block of 8 rows (0 to 7, 8 to 15, ...) at most 4 rows name the same one
- edge_target: int32 [32], P('edge'), may hold values from 0 to 23
- edge_counts: int32 [4], P('edge'), may hold values from 4 to 8, as said below
- corr_weight: bfloat16 [49, 128], replicated, may hold values from -0.875 to 0.875
- gate_weight: bfloat16 [3, 3, 256, 256], replicated, may hold values from -0.125 to 0.125
- candidate_weight: bfloat16 [3, 3, 256, 128], replicated, may hold values from -0.125 to 0.125
- jacobian_weight: bfloat16 [128, 24], replicated, may hold values from -0.5 to 0.5
- confidence_weight: bfloat16 [128, 2], replicated, may hold values from -3 to 3
Outputs:
- hidden_next: bfloat16 [32, 48, 64, 128], P('edge', 'tile')
- camera_hessian: float32 [576, 576], P('tile', 'edge')
- pose_diagonal: float32 [96, 36], P('edge')
Inputs may be any that keep to these rules, and one draw needn't show every extreme that they name: `edge_owner`: in the rows of one index of edge at most 4 edges name the same owner, a bound that some block reaches. `edge_counts`: edges past a device's count are unused; some index of edge uses all 8.
All inputs are finite; a program needn't handle non-finite values.
Results may differ from a plain program's by a relative error of at most 0.015.
Values may be sent and summed in bfloat16 or wider, within the bound.
A program may use at most 128 MiB of HBM per device.

v0:
```python
import jax
import jax.numpy as jnp
from jax import lax
from jax.sharding import PartitionSpec as P

MAPH = 48
MAPW = 64
WINDOW = 7


def padded_2(cells, sides, width):
    for axis, dim in sides:
        count = lax.axis_size(axis)
        ends = count - 1
        head = lax.slice_in_dim(cells, 0, width, axis=dim)
        tail = lax.slice_in_dim(cells, cells.shape[dim] - width, cells.shape[dim], axis=dim)
        cells = jnp.concatenate(
            [
                lax.ppermute(tail, axis, [(i, (i + 1) % count) for i in range(ends)]),
                cells,
                lax.ppermute(head, axis, [((i + 1) % count, i) for i in range(ends)]),
            ],
            axis=dim,
        )
    return cells


def pad_columns(values):
    return jnp.pad(values, ((0, 0), (0, 0), (1, 1), (0, 0)))


def convolve(padded, weight):
    row_count = padded.shape[1] - 2
    col_count = padded.shape[2] - 2
    running = jnp.zeros((padded.shape[0], row_count, col_count, weight.shape[-1]), jnp.float32)
    for row_step in range(3):
        for col_step in range(3):
            window = padded[:, row_step : row_step + row_count, col_step : col_step + col_count]
            running = running + jnp.einsum(
                "erwc,ck->erwk",
                window,
                weight[row_step, col_step],
                preferred_element_type=jnp.float32,
            )
    return running


def per_device(
    features,
    hidden_state,
    edge_source,
    edge_owner,
    edge_target,
    edge_counts,
    corr_weight,
    gate_weight,
    candidate_weight,
    jacobian_weight,
    confidence_weight,
):
    edge_total = hidden_state.shape[0]
    frame_total = features.shape[0]
    band_rows = features.shape[1]
    map_width = features.shape[2]
    hidden_width = hidden_state.shape[3]
    owner_count = lax.axis_size("edge")
    slot_depth = max(2, (2 * edge_total + owner_count - 1) // owner_count)
    my_index = lax.axis_index("edge")
    in_use = jnp.arange(edge_total) < edge_counts[0]
    owners = edge_owner[:, 0]
    owner_hits = (owners[:, None] == jnp.arange(owner_count)[None, :]).astype(jnp.int32)
    earlier = jnp.cumsum(owner_hits, axis=0) - owner_hits
    rank_within = jnp.sum(earlier * owner_hits, axis=1)
    slot_index = owners * slot_depth + rank_within
    slot_hits = (slot_index[:, None] == jnp.arange(owner_count * slot_depth)[None, :]).astype(
        jnp.int32
    )
    source_global = my_index * frame_total + edge_source
    target_global = owners * frame_total + edge_target
    send_target = jnp.sum(slot_hits * edge_target[:, None], axis=0).reshape(owner_count, slot_depth)
    send_source = jnp.sum(slot_hits * source_global[:, None], axis=0).reshape(
        owner_count, slot_depth
    )
    got_target, got_source = (
        lax.all_to_all(send_target, "edge", split_axis=0, concat_axis=0, tiled=True),
        lax.all_to_all(send_source, "edge", split_axis=0, concat_axis=0, tiled=True),
    )
    asked = jnp.take(features, got_target.reshape(-1), axis=0).reshape(
        (owner_count, slot_depth) + features.shape[1:]
    )
    returned = lax.all_to_all(asked, "edge", split_axis=0, concat_axis=0, tiled=True)
    target_maps = jnp.take(
        returned.reshape((owner_count * slot_depth,) + features.shape[1:]), slot_index, axis=0
    )
    radius = WINDOW // 2
    source_maps = jnp.take(features, edge_source, axis=0)
    target_rows = padded_2(target_maps, (("tile", 1),), radius)
    target_padded = jnp.pad(target_rows, ((0, 0), (0, 0), (radius, radius), (0, 0)))
    columns = []
    for row_shift in range(WINDOW):
        for col_shift in range(WINDOW):
            moved = target_padded[
                :, row_shift : row_shift + band_rows, col_shift : col_shift + map_width
            ]
            columns.append(
                jnp.einsum("erwh,erwh->erw", source_maps, moved, preferred_element_type=jnp.float32)
            )
    corr = (jnp.stack(columns, axis=-1) * features.shape[3] ** (-0.5)).astype(jnp.bfloat16)
    motion = jax.nn.relu(
        jnp.einsum("ercd,dk->erck", corr, corr_weight, preferred_element_type=jnp.float32)
    ).astype(jnp.bfloat16)
    stacked = jnp.concatenate([hidden_state, motion], axis=-1)
    state_float = hidden_state.astype(jnp.float32)
    extended = padded_2(stacked, (("tile", 1),), 1)
    gates = jax.nn.sigmoid(convolve(pad_columns(extended), gate_weight))
    update = gates[..., :hidden_width]
    reset_state = (gates[..., hidden_width:] * state_float).astype(jnp.bfloat16)
    mixed = jnp.concatenate([reset_state, motion], axis=-1)
    mixed_extended = padded_2(mixed, (("tile", 1),), 1)
    candidate = jnp.tanh(convolve(pad_columns(mixed_extended), candidate_weight))
    new_state = ((1.0 - update) * state_float + update * candidate).astype(jnp.bfloat16)
    hidden_next = jnp.where(in_use[:, None, None, None], new_state, hidden_state)
    pixel_total = band_rows * map_width
    jacobian = jnp.einsum(
        "erwh,hk->ekrw", new_state, jacobian_weight, preferred_element_type=jnp.float32
    ).reshape(edge_total, 2, 12, pixel_total)
    confidence = jax.nn.softplus(
        jnp.einsum(
            "erwh,hk->ekrw", new_state, confidence_weight, preferred_element_type=jnp.float32
        )
    ).reshape(edge_total, 2, 1, pixel_total)
    normal_blocks = jnp.einsum(
        "ekap,ekbp->eab", jacobian * confidence, jacobian, precision=lax.Precision.HIGHEST
    ) / (MAPH * MAPW)
    normal_blocks = normal_blocks * in_use.astype(jnp.float32)[:, None, None]
    outgoing = jnp.concatenate(
        [
            normal_blocks[:, 6:, 6:].reshape(edge_total, 36),
            normal_blocks[:, :6, 6:].reshape(edge_total, 36),
        ],
        axis=1,
    )
    slot_blocks = jnp.einsum(
        "es,eq->sq", slot_hits.astype(jnp.float32), outgoing, precision=lax.Precision.HIGHEST
    ).reshape(owner_count, slot_depth, 72)
    incoming = lax.all_to_all(slot_blocks, "edge", split_axis=0, concat_axis=0, tiled=True).reshape(
        owner_count * slot_depth, 72
    )
    flat_target = got_target.reshape(-1)
    flat_source = got_source.reshape(-1)
    row_frames = jnp.concatenate(
        [source_global, target_global, my_index * frame_total + flat_target, flat_source]
    )
    col_frames = jnp.concatenate([edge_source, edge_source, flat_target, flat_target])
    block_list = jnp.concatenate(
        [
            normal_blocks[:, :6, :6],
            normal_blocks[:, 6:, :6],
            incoming[:, :36].reshape(-1, 6, 6),
            incoming[:, 36:].reshape(-1, 6, 6),
        ],
        axis=0,
    )
    on_diagonal = (row_frames == my_index * frame_total + col_frames).astype(jnp.float32)
    col_hits = (col_frames[:, None] == jnp.arange(frame_total)[None, :]).astype(jnp.float32)
    diagonal_part = jnp.einsum(
        "if,iq->fq",
        col_hits * on_diagonal[:, None],
        block_list.reshape(-1, 36),
        precision=lax.Precision.HIGHEST,
    )
    apart_blocks = block_list * (1.0 - on_diagonal)[:, None, None]
    spread = (apart_blocks[:, :, None, :] * col_hits[:, None, :, None]).reshape(
        -1, 6, frame_total * 6
    )
    own_rows = frame_total * owner_count * 6 // lax.axis_size("tile")
    frame_span = own_rows * lax.axis_size("tile") // 6
    row_hits = (row_frames[:, None] == jnp.arange(frame_span)[None, :]).astype(jnp.float32)
    placed = jnp.einsum("ic,ixq->cxq", row_hits, spread, precision=lax.Precision.HIGHEST)
    camera_hessian = lax.psum_scatter(
        placed.reshape(own_rows * lax.axis_size("tile"), frame_total * 6).astype(jnp.bfloat16),
        "tile",
        scatter_dimension=0,
        tiled=True,
    ).astype(jnp.float32)
    pose_diagonal = lax.psum(diagonal_part, "tile")
    return (hidden_next, camera_hessian, pose_diagonal)


def solution(mesh):
    placed = (
        P("edge", "tile", None, None),
        P("edge", "tile", None, None),
        P("edge"),
        P("edge", None),
        P("edge"),
        P("edge"),
        P(),
        P(),
        P(),
        P(),
        P(),
    )
    return jax.shard_map(
        per_device,
        mesh=mesh,
        in_specs=placed,
        out_specs=(P("edge", "tile", None, None), P("tile", "edge"), P("edge", None)),
        check_vma=False,
    )
```

profile of v0, /device:TPU:0, one launch (start us, length us, event | category | flops | bytes accessed | tf_op | source)
XLA Modules:
  0.0 204.7 jit_solution(6177645534464706526)
XLA Ops:
  7.2 0.8 fusion.173
  8.2 0.7 select_reduce_fusion.2
  8.9 0.7 fusion.198
  10.2 0.7 select_reduce_fusion
  11.0 9.7 %all_to_all.28 = s32[4,1,4]{2,1,0:T(1,128)S(1)} all-to-all(s32[4,1,4]{2,1,0:T(1,128)S(1)} %bitcast.304), channel_id=1, replica_groups=mesh['edge'=4,'tile'=8] {'edge'}, dimensions={0} | all-to-all | bytes 128 | tf_op jit(solution)/shard_map/all_to_all | solution.py:85
  21.2 0.7 reduce.106
  22.0 1.9 gather_fusion.1
  23.9 2.8 %broadcast_select_fusion = bf16[4,4,6,64,128]{4,3,2,1,0:T(8,128)(2,1)} fusion(bf16[4,4,6,64,128]{4,3,2,1,0:T(8,128)(2,1)} %bitcast.251, pred[4,4]{1,0:T(4,128)(4,1)S(1)} %compare_and_fusion), kind=kLoop, calls=%fused_computation.176 | loop fusion | flops 786432 | bytes 3145744 | tf_op jit(solution)/shard_map/jit(_take)/select_n | solution.py:88
  26.6 4.3 %all-to-all-start.1 = ((bf16[4,4,6,64,128]{4,3,2,1,0:T(8,128)(2,1)}), bf16[4,4,6,64,128]{4,3,2,1,0:T(8,128)(2,1)}, u32[]{:S(2)}, u32[]{:S(2)}) async-start(bf16[4,4,6,64,128]{4,3,2,1,0:T(8,128)(2,1)} %broadcast_select_fusion), calls=%async_computation.1 | async-start | bytes 3145728 | tf_op jit(solution)/shard_map/all_to_all | solution.py:91
  31.0 0.7 gather_fusion
  32.4 0.7 all_to_all.21
  33.7 15.4 %all-to-all-done.1 = bf16[4,4,6,64,128]{4,3,2,1,0:T(8,128)(2,1)} async-done(((bf16[4,4,6,64,128]{4,3,2,1,0:T(8,128)(2,1)}), bf16[4,4,6,64,128]{4,3,2,1,0:T(8,128)(2,1)}, u32[]{:S(2)}, u32[]{:S(2)}) %all-to-all-start.1) | async-done | bytes 1572896 | tf_op jit(solution)/shard_map/all_to_all | solution.py:91
  49.1 3.2 %all-to-all-start.2 = ((s32[4,1,4]{2,1,0:T(1,128)}), s32[4,1,4]{2,1,0:T(1,128)S(1)}, u32[]{:S(2)}, u32[]{:S(2)}) async-start(s32[4,1,4]{2,1,0:T(1,128)} %bitcast.116), calls=%async_computation.2 | async-start | bytes 4096 | tf_op jit(solution)/shard_map/all_to_all | solution.py:86
  52.4 2.1 %gather_fusion.2 = bf16[8,6,64,128]{3,2,1,0:T(8,128)(2,1)S(1)} fusion(bf16[16,6,64,128]{3,2,1,0:T(8,128)(2,1)} %bitcast.9, s32[1024]{0:T(1024)S(1)} %pad_clamp_fusion), kind=kCustom, calls=%fused_computation.2 | custom fusion | bytes 1572896 | tf_op jit(solution)/shard_map/jit(_take)/gather | solution.py:92
  54.7 1.3 collective-permute-start
  56.0 1.3 collective-permute-start.1
  57.9 0.7 reduce.107
  59.3 2.1 %collective-permute-done.1 = bf16[8,3,64,128]{3,2,1,0:T(8,128)(2,1)S(1)} collective-permute-done((bf16[8,3,64,128]{3,2,1,0:T(8,128)(2,1)S(1)}, bf16[8,3,64,128]{3,2,1,0:T(8,128)(2,1)S(1)}, u32[]{:S(2)}, u32[]{:S(2)}) %collective-permute-start.1) | collective-permute-done | bytes 393248 | tf_op jit(solution)/shard_map/ppermute | solution.py:21
  61.4 1.0 fusion.29
  62.4 7.7 %fusion.75 = (f32[8,6,64]{2,1,0:T(8,128)S(1)}, f32[8,6,64]{2,1,0:T(8,128)S(1)}, f32[8,6,64]{2,1,0:T(8,128)S(1)}, f32[8,6,64]{2,1,0:T(8,128)S(1)}, f32[8,6,64]{2,...) fusion(bf16[8,12,70,128]{3,2,1,0:T(8,128)(2,1)S(1)} %fusion.29,, ...), kind=kLoop, calls=%fused_computation.154 | loop fusion | flops 20788224 | bytes 14364680
  70.1 7.6 %fusion.95 = (f32[8,6,64]{2,1,0:T(8,128)S(1)}, f32[8,6,64]{2,1,0:T(8,128)S(1)}, f32[8,6,64]{2,1,0:T(8,128)S(1)}, f32[8,6,64]{2,1,0:T(8,128)S(1)}, f32[8,6,64]{2,...) fusion(bf16[8,12,70,128]{3,2,1,0:T(8,128)(2,1)S(1)} %fusion.29,, ...), kind=kLoop, calls=%fused_computation.174 | loop fusion | flops 20788224 | bytes 14364680
  77.8 3.6 %fusion.55 = (f32[8,6,64]{2,1,0:T(8,128)S(1)}, f32[8,6,64]{2,1,0:T(8,128)S(1)}, f32[8,6,64]{2,1,0:T(8,128)S(1)}, f32[8,6,64]{2,1,0:T(8,128)S(1)}, f32[8,6,64]{2,...) fusion(bf16[8,12,70,128]{3,2,1,0:T(8,128)(2,1)S(1)} %fusion.29, ...), kind=kLoop, calls=%fused_computation.134 | loop fusion | flops 10199040 | bytes 7176200
  89.4 3.4 %fusion.92 = (f32[8,6,64]{2,1,0:T(8,128)S(1)}, f32[8,6,64]{2,1,0:T(8,128)S(1)}, f32[8,6,64]{2,1,0:T(8,128)S(1)}, f32[8,6,64]{2,1,0:T(8,128)S(1)}, f32[8,6,64]{2,...) fusion(bf16[8,3,64,128]{3,2,1,0:T(8,128)(2,1)S(1)} %collective-permute-done.1, ...), kind=kLoop, calls=%fused_computation.171 | loop fusion | flops 11381760 | bytes 2445320
  93.0 8.1 %stack.199 = f32[8,6,64,49]{2,3,1,0:T(8,128)} concatenate(f32[8,6,64,1]{2,3,1,0:T(1,128)} %copy.199, f32[8,6,64,1]{2,3,1,0:T(1,128)} %copy.200, f32[8,6,64,1]{2,3,1,0:T(1,128)} %copy.201, f32[8,6,64,1]{2,3,1,0:T(1,128)S(1)} %copy.202, f32[8,6,64,1]{2,3,1,0:T(1,128)} %copy.203, f32[8,6,64,1]{2,3,1,0:T(1,128)} %copy.204, f32[8,6,64,1]{2,3,1,0:T(1,128)} %copy.205, ...), dimensions={3} | concatenate | bytes 1204224 | tf_op jit(solution)/shard_map/stack | solution.py:108
  101.1 1.8 maximum_convert_fusion
  103.1 8.0 %collective-permute-start.2 = (bf16[8,1,64,256]{3,2,1,0:T(8,128)(2,1)S(1)}, bf16[8,1,64,256]{3,2,1,0:T(8,128)(2,1)S(1)}, u32[]{:S(2)}, u32[]{:S(2)}) collective-permute-start(bf16[8,1,64,256]{3,2,1,0:T(8,128)(2,1)S(1)} %get-tuple-element.63), channel_id=1, source_target_pairs={{0,1},{1,2},{2,3},{3,4},{4,5},{5,6},{6,7},{8,9},{9,10},{10,11},{11... | collective-permute-start | bytes 786440 | tf_op jit(solution)/shard_map/ppermute | solution.py:19
  111.1 1.3 collective-permute-start.3
  113.0 1.5 collective-permute-done.3
  117.8 2.2 %fusion.15 = f32[8,6,64,256]{3,2,1,0:T(8,128)} fusion(bf16[8,6,64,128]{3,2,1,0:T(8,128)(2,1)S(1)} %maximum_convert_fusion, bf16[8,6,64,128]{3,2,1,0:T(8,128)(2,1)S(1)} %copy-done.2, bf16[8,1,64,256]{3,2,1,0:T(8,128)(2,1)S(1)} %collective-permute-done.2, bf16[3,3,256,256]{3,2,1,0:T(8,128)(2,1)S(1)} %copy-done.4), kind=kOutput, calls=%fused_computation.84 | convolution fusion | flops 408158208 | bytes 5111808 | tf_op jit(solution)/shard_map/erwc,ck->erwk/dot_general | solution.py:39
  120.0 2.3 %fusion.9 = f32[8,6,64,256]{3,2,1,0:T(8,128)} fusion(bf16[8,6,64,128]{3,2,1,0:T(8,128)(2,1)S(1)} %maximum_convert_fusion, bf16[8,1,64,256]{3,2,1,0:T(8,128)(2,1)S(1)} %collective-permute-done.3, bf16[8,6,64,128]{3,2,1,0:T(8,128)(2,1)S(1)} %copy-done.2, bf16[3,3,256,256]{3,2,1,0:T(8,128)(2,1)S(1)} %copy-done.4), kind=kOutput, calls=%fused_computation.80 | convolution fusion | flops 408158208 | bytes 5111808 | tf_op jit(solution)/shard_map/erwc,ck->erwk/dot_general | solution.py:39
  122.3 5.2 %add_divide_fusion = f32[8,6,64,256]{3,2,1,0:T(8,128)} fusion(f32[8,6,64,256]{3,2,1,0:T(8,128)} %fusion.9, f32[8,6,64,256]{3,2,1,0:T(8,128)S(1)} %fusion.34, f32[8,6,64,256]{3,2,1,0:T(8,128)S(1)} %fusion.33, f32[8,6,64,256]{3,2,1,0:T(8,128)S(1)} %fusion.45, f32[8,6,64,256]{3,2,1,0:T(8,128)S(1)} %fusion.32, f32[8,6,64,256]{3,2,1,0:T(8,128)S(1)} %fusion.31, ...), kind=kOutput, calls=%fused_computation.55 | convolution fusion | flops 411303936 | bytes 30539776 | tf_op jit(solution)/shard_map/erwc,ck->erwk/dot_general | solution.py:39
  127.5 1.7 fusion.44
  129.3 6.3 %collective-permute-start.4 = (bf16[8,1,64,256]{3,2,1,0:T(8,128)(2,1)S(1)}, bf16[8,1,64,256]{3,2,1,0:T(8,128)(2,1)S(1)}, u32[]{:S(2)}, u32[]{:S(2)}) collective-permute-start(bf16[8,1,64,256]{3,2,1,0:T(8,128)(2,1)S(1)} %get-tuple-element.61), channel_id=1, source_target_pairs={{0,1},{1,2},{2,3},{3,4},{4,5},{5,6},{6,7},{8,9},{9,10},{10,11},{11... | collective-permute-start | bytes 786440 | tf_op jit(solution)/shard_map/ppermute | solution.py:19
  135.6 1.5 collective-permute-start.5
  137.7 1.3 collective-permute-done.5
  143.4 1.3 copy-done.3
  144.7 2.3 %broadcast_select_fusion.3 = (bf16[8,6,64,128]{3,2,1,0:T(8,128)(2,1)}, bf16[8,6,64,128]{3,2,1,0:T(8,128)(2,1)S(1)}) fusion(bf16[8,6,64,128]{3,2,1,0:T(8,128)(2,1)S(1)} %copy-done.2, pred[8]{0:T(512)(128)(4,1)S(1)} %copy-done.15, bf16[3,3,256,128]{3,2,1,0:T(8,128)(2,1)S(1)} %copy-done.5, bf16[8,8,64,256]{3,2,1,0:T(8,128)(2,1)S(1)} %fusion.4, ...), kind=kOutput, calls=%fused_computation.199 | convolution fusion | flops 207224832 | bytes 18678272 | tf_op jit(solution)/shard_map/erwc,ck->erwk/dot_general | solution.py:39
  147.0 0.7 convolution_bitcast_fusion
  148.4 0.7 compare_select_fusion
  150.1 0.9 fusion.166
  151.0 4.2 %all-to-all-start.3 = ((f32[4,4,72]{2,1,0:T(4,128)}), f32[4,4,72]{2,1,0:T(4,128)S(1)}, u32[]{:S(2)}, u32[]{:S(2)}) async-start(f32[4,4,72]{2,1,0:T(4,128)} %bitcast.126), calls=%async_computation.3 | async-start | bytes 16384 | tf_op jit(solution)/shard_map/all_to_all | solution.py:146
  155.5 4.4 %all-to-all-done.3 = f32[4,4,72]{2,1,0:T(4,128)S(1)} async-done(((f32[4,4,72]{2,1,0:T(4,128)}), f32[4,4,72]{2,1,0:T(4,128)S(1)}, u32[]{:S(2)}, u32[]{:S(2)}) %all-to-all-start.3) | async-done | bytes 4640 | tf_op jit(solution)/shard_map/all_to_all | solution.py:146
  160.4 1.1 convolution_convert_fusion
  161.4 1.3 copy.258
  162.7 0.9 convert_element_type.73
  163.9 28.7 %psum.7 = f32[24,36]{1,0:T(8,128)} all-reduce(f32[24,36]{1,0:T(8,128)S(1)} %fusion.148), channel_id=1, replica_groups=mesh['edge'=4,'tile'=8] {'tile'}, use_global_device_ids=true, to_apply=%region_5.6 | all-reduce | flops 864 | bytes 6912 | tf_op jit(solution)/shard_map/psum | solution.py:186
  192.6 3.9 %reduce-scatter.2.cloned.1.call-done = bf16[72,144]{1,0:T(8,128)(2,1)} async-done(((bf16[576,144]{1,0:T(8,128)(2,1)}), bf16[72,144]{1,0:T(8,128)(2,1)}) %reduce-scatter.2.cloned.1.call-update) | async-done | bytes 20752 | tf_op jit(solution)/shard_map/reduce_scatter | solution.py:180
  196.5 1.4 convert_element_type.74
  (158 shorter events, 23.1 us)
Async XLA Ops:
  7.2 14.8 %copy-start = (bf16[24,6,64,128]{3,2,1,0:T(8,128)(2,1)S(1)}, bf16[24,6,64,128]{3,2,1,0:T(8,128)(2,1)}, u32[]{:S(2)}) copy-start(bf16[24,6,64,128]{3,2,1,0:T(8,128)(2,1)} %param.11) | copy-start | bytes 7077892
  26.6 22.5 %all-to-all-start.1 = ((bf16[4,4,6,64,128]{4,3,2,1,0:T(8,128)(2,1)}), bf16[4,4,6,64,128]{4,3,2,1,0:T(8,128)(2,1)}, u32[]{:S(2)}, u32[]{:S(2)}) async-start(bf16[4,4,6,64,128]{4,3,2,1,0:T(8,128)(2,1)} %broadcast_select_fusion), calls=%async_computation.1 | async-start | bytes 3145728 | tf_op jit(solution)/shard_map/all_to_all | solution.py:91
  31.0 2.7 %copy-start.14 = (s32[8]{0:T(128)S(1)}, s32[8]{0:T(128)}, u32[]{:S(2)}) copy-start(s32[8]{0:T(128)} %param.13) | copy-start | bytes 100
  31.0 2.7 %copy-start.11 = (s32[8,1]{0,1:T(1,128)S(1)}, s32[8,1]{0,1:T(1,128)}, u32[]{:S(2)}) copy-start(s32[8,1]{0,1:T(1,128)} %param.14) | copy-start | bytes 100
  31.0 2.7 %copy-start.17 = (s32[8]{0:T(128)S(1)}, s32[8]{0:T(128)}, u32[]{:S(2)}) copy-start(s32[8]{0:T(128)} %param.15) | copy-start | bytes 100
  49.1 8.8 %all-to-all-start.2 = ((s32[4,1,4]{2,1,0:T(1,128)}), s32[4,1,4]{2,1,0:T(1,128)S(1)}, u32[]{:S(2)}, u32[]{:S(2)}) async-start(s32[4,1,4]{2,1,0:T(1,128)} %bitcast.116), calls=%async_computation.2 | async-start | bytes 4096 | tf_op jit(solution)/shard_map/all_to_all | solution.py:86
  54.7 4.6 %collective-permute-start = (bf16[8,3,64,128]{3,2,1,0:T(8,128)(2,1)S(1)}, bf16[8,3,64,128]{3,2,1,0:T(8,128)(2,1)S(1)}, u32[]{:S(2)}, u32[]{:S(2)}) collective-permute-start(bf16[8,3,64,128]{3,2,1,0:T(8,128)(2,1)S(1)} %get-tuple-element.65), channel_id=1, source_target_pairs={{0,1},{1,2},{2,3},{3,4},{4,5},{5,6},{6,7},{8,9},{9,10},{10,11},{11... | collective-permute-start | bytes 1179656 | tf_op jit(solution)/shard_map/ppermute | solution.py:19
  56.0 5.4 %collective-permute-start.1 = (bf16[8,3,64,128]{3,2,1,0:T(8,128)(2,1)S(1)}, bf16[8,3,64,128]{3,2,1,0:T(8,128)(2,1)S(1)}, u32[]{:S(2)}, u32[]{:S(2)}) collective-permute-start(bf16[8,3,64,128]{3,2,1,0:T(8,128)(2,1)S(1)} %get-tuple-element.66), channel_id=1, source_target_pairs={{1,0},{2,1},{3,2},{4,3},{5,4},{6,5},{7,6},{9,8},{10,9},{11,10},{12... | collective-permute-start | bytes 1179656 | tf_op jit(solution)/shard_map/ppermute | solution.py:21
  88.1 4.9 %copy-start.6 = (f32[8,6,64,1]{2,3,1,0:T(1,128)S(1)}, f32[8,6,64,1]{2,3,1,0:T(1,128)}, u32[]{:S(2)}) copy-start(f32[8,6,64,1]{2,3,1,0:T(1,128)} %copy.227) | copy-start | bytes 36868
  88.1 4.9 %copy-start.7 = (f32[8,6,64,1]{2,3,1,0:T(1,128)S(1)}, f32[8,6,64,1]{2,3,1,0:T(1,128)}, u32[]{:S(2)}) copy-start(f32[8,6,64,1]{2,3,1,0:T(1,128)} %copy.228) | copy-start | bytes 36868
  88.1 4.9 %copy-start.8 = (f32[8,6,64,1]{2,3,1,0:T(1,128)S(1)}, f32[8,6,64,1]{2,3,1,0:T(1,128)}, u32[]{:S(2)}) copy-start(f32[8,6,64,1]{2,3,1,0:T(1,128)} %copy.229) | copy-start | bytes 36868
  92.7 8.4 %copy-start.9 = (bf16[49,128]{1,0:T(8,128)(2,1)S(1)}, bf16[49,128]{1,0:T(8,128)(2,1)}, u32[]{:S(2)}) copy-start(bf16[49,128]{1,0:T(8,128)(2,1)} %param.17) | copy-start | bytes 37636
  101.1 1.8 copy-start.2
  103.0 9.4 %copy-start.4 = (bf16[3,3,256,256]{3,2,1,0:T(8,128)(2,1)S(1)}, bf16[3,3,256,256]{3,2,1,0:T(8,128)(2,1)}, u32[]{:S(2)}) copy-start(bf16[3,3,256,256]{3,2,1,0:T(8,128)(2,1)} %param.18) | copy-start | bytes 3538948
  103.1 9.9 %collective-permute-start.2 = (bf16[8,1,64,256]{3,2,1,0:T(8,128)(2,1)S(1)}, bf16[8,1,64,256]{3,2,1,0:T(8,128)(2,1)S(1)}, u32[]{:S(2)}, u32[]{:S(2)}) collective-permute-start(bf16[8,1,64,256]{3,2,1,0:T(8,128)(2,1)S(1)} %get-tuple-element.63), channel_id=1, source_target_pairs={{0,1},{1,2},{2,3},{3,4},{4,5},{5,6},{6,7},{8,9},{9,10},{10,11},{11... | collective-permute-start | bytes 786440 | tf_op jit(solution)/shard_map/ppermute | solution.py:19
  111.1 3.4 %collective-permute-start.3 = (bf16[8,1,64,256]{3,2,1,0:T(8,128)(2,1)S(1)}, bf16[8,1,64,256]{3,2,1,0:T(8,128)(2,1)S(1)}, u32[]{:S(2)}, u32[]{:S(2)}) collective-permute-start(bf16[8,1,64,256]{3,2,1,0:T(8,128)(2,1)S(1)} %get-tuple-element.64), channel_id=1, source_target_pairs={{1,0},{2,1},{3,2},{4,3},{5,4},{6,5},{7,6},{9,8},{10,9},{11,10},{12... | collective-permute-start | bytes 786440 | tf_op jit(solution)/shard_map/ppermute | solution.py:21
  129.2 7.9 %copy-start.5 = (bf16[3,3,256,128]{3,2,1,0:T(8,128)(2,1)S(1)}, bf16[3,3,256,128]{3,2,1,0:T(8,128)(2,1)}, u32[]{:S(2)}) copy-start(bf16[3,3,256,128]{3,2,1,0:T(8,128)(2,1)} %param.19) | copy-start | bytes 1769476
  129.3 8.4 %collective-permute-start.4 = (bf16[8,1,64,256]{3,2,1,0:T(8,128)(2,1)S(1)}, bf16[8,1,64,256]{3,2,1,0:T(8,128)(2,1)S(1)}, u32[]{:S(2)}, u32[]{:S(2)}) collective-permute-start(bf16[8,1,64,256]{3,2,1,0:T(8,128)(2,1)S(1)} %get-tuple-element.61), channel_id=1, source_target_pairs={{0,1},{1,2},{2,3},{3,4},{4,5},{5,6},{6,7},{8,9},{9,10},{10,11},{11... | collective-permute-start | bytes 786440 | tf_op jit(solution)/shard_map/ppermute | solution.py:19
  135.6 3.4 %collective-permute-start.5 = (bf16[8,1,64,256]{3,2,1,0:T(8,128)(2,1)S(1)}, bf16[8,1,64,256]{3,2,1,0:T(8,128)(2,1)S(1)}, u32[]{:S(2)}, u32[]{:S(2)}) collective-permute-start(bf16[8,1,64,256]{3,2,1,0:T(8,128)(2,1)S(1)} %get-tuple-element.62), channel_id=1, source_target_pairs={{1,0},{2,1},{3,2},{4,3},{5,4},{6,5},{7,6},{9,8},{10,9},{11,10},{12... | collective-permute-start | bytes 786440 | tf_op jit(solution)/shard_map/ppermute | solution.py:21
  142.8 1.9 copy-start.3
  142.8 1.9 copy-start.15
  144.7 2.3 %copy-start.10 = (bf16[128,24]{0,1:T(8,128)(2,1)S(1)}, bf16[128,24]{0,1:T(8,128)(2,1)}, u32[]{:S(2)}) copy-start(bf16[128,24]{0,1:T(8,128)(2,1)} %param.20) | copy-start | bytes 18436
  147.7 0.7 copy-start.19
  147.9 1.4 copy-start.16
  148.4 6.8 %copy-start.12 = (s32[48]{0:T(128)S(1)}, s32[48]{0:T(128)}, u32[]{:S(2)}) copy-start(s32[48]{0:T(128)} %get-tuple-element.59) | copy-start | bytes 580
  151.0 8.9 %all-to-all-start.3 = ((f32[4,4,72]{2,1,0:T(4,128)}), f32[4,4,72]{2,1,0:T(4,128)S(1)}, u32[]{:S(2)}, u32[]{:S(2)}) async-start(f32[4,4,72]{2,1,0:T(4,128)} %bitcast.126), calls=%async_computation.3 | async-start | bytes 16384 | tf_op jit(solution)/shard_map/all_to_all | solution.py:146
  155.2 41.3 %reduce-scatter.2.cloned.1.call-start = ((), (), s32[]{:S(2)}) async-start(), calls=%async_computation.5 | async-start | bytes 331776 | tf_op jit(solution)/shard_map/reduce_scatter | solution.py:180
  160.2 37.7 %copy-start.1 = (bf16[24,6,64,128]{3,2,1,0:T(8,128)(2,1)S(1)}, bf16[24,6,64,128]{3,2,1,0:T(8,128)(2,1)}, u32[]{:S(2)}) copy-start(bf16[24,6,64,128]{3,2,1,0:T(8,128)(2,1)} %param.11) | copy-start | bytes 7077892
  160.3 3.5 %copy-start.13 = (s32[48]{0:T(128)S(1)}, s32[48]{0:T(128)}, u32[]{:S(2)}) copy-start(s32[48]{0:T(128)} %get-tuple-element.59) | copy-start | bytes 580
  160.4 3.4 %copy-start.18 = (f32[48]{0:T(128)S(1)}, f32[48]{0:T(128)}, u32[]{:S(2)}) copy-start(f32[48]{0:T(128)} %get-tuple-element.58) | copy-start | bytes 580
Sparse Core Ops, SparseCore 0:
  163.7 32.7 reduce-scatter.1
where the time goes:
time: 206 us; the launch traced here: 205 us
  blocking collectives  38.4 us (19%)
  other arithmetic  36.9 us (18%)
  starting transfers between devices  31.5 us (15%)
  waiting for transfers between devices  28.7 us (14%)
  local copies, waits for them, and re-layouts  27.6 us (13%)
  matrix products  26.1 us (13%)
  between operations  15.6 us (8%)
    psum x1, blocking collectives, per_device(): pose_diagonal = lax.psum(diagonal_part, 'tile')  28.7 us
    unnamed x4, other arithmetic  22.3 us
    dot_general x18, matrix products, convolve(): jnp.einsum('erwc,ck->erwk', window, weight[row_step, col_step], preferred...  20.2 us
    another operation x50, local copies, waits for them, and re-layouts, per_device(): jnp.stack(columns, axis=-1) * features.shape[3] ** (-0.5)  16 us
    ppermute x3, starting transfers between devices, padded_2(): lax.ppermute(tail, axis, [(i, (i + 1) % count) for i in range(ends)])  15.7 us
    all_to_all x1, waiting for transfers between devices, per_device(): lax.all_to_all(asked, 'edge', split_axis=0, concat_axis=0, tiled=True)  15.4 us
    all_to_all x1, blocking collectives, per_device(): lax.all_to_all(send_target, 'edge', split_axis=0, concat_axis=0, tiled=True)  9.66 us
    ppermute x3, waiting for transfers between devices, padded_2(): lax.ppermute(head, axis, [((i + 1) % count, i) for i in range(ends)])  4.95 us
  transfers between devices with their start and end apart: 10, of which 6 were waited for; matrix products, arithmetic and copies ran while one was open for 4% of the time, Pallas kernels for 0%

commit v1 on v0

--- a/solution.py
+++ b/solution.py
@@ -183,7 +183,11 @@
         scatter_dimension=0,
         tiled=True,
     ).astype(jnp.float32)
-    pose_diagonal = lax.psum(diagonal_part, "tile")
+    pose_diagonal = diagonal_part
+    for hop in (1, 2, 4):
+        pose_diagonal = pose_diagonal + lax.ppermute(
+            pose_diagonal, "tile", [(dev, dev ^ hop) for dev in range(8)]
+        )
     return (hidden_next, camera_hessian, pose_diagonal)
 
 

time: 206 us -> 206 us (level)
  blocking collectives: 38.4 us -> 9.66 us
  waiting for transfers between devices: 28.7 us -> 49.6 us
  starting transfers between devices: 31.5 us -> 38.5 us
    psum x1 -> x0, blocking collectives: 28.7 us -> none  [per_device(): pose_diagonal = lax.psum(diagonal_part, 'tile')]
    reduce_scatter x1, waiting for transfers between devices: 3.85 us -> 19.8 us  [per_device(): lax.psum_scatter(placed.reshape(own_rows * lax.axis_size('tile'), frame_t...]
    ppermute x0 -> x3, starting transfers between devices: none -> 7.05 us  [per_device(): lax.ppermute(pose_diagonal, 'tile', [(dev, dev ^ hop) for dev in range(8)])]
    ppermute x0 -> x3, waiting for transfers between devices: none -> 4.98 us  [per_device(): lax.ppermute(pose_diagonal, 'tile', [(dev, dev ^ hop) for dev in range(8)])]
  transfers between devices with their start and end apart: 10 -> 13, of which waited for: 6 -> 9; matrix products, arithmetic and copies ran while one was open for 4% -> 4% of each run, Pallas kernels for 0% -> 0%
where the time goes in v1:
time: 206 us; the launch traced here: 205 us
  waiting for transfers between devices  49.6 us (24%)
  starting transfers between devices  38.5 us (19%)
  other arithmetic  37.6 us (18%)
  local copies, waits for them, and re-layouts  27.6 us (13%)
  matrix products  26.1 us (13%)
  between operations  15.6 us (8%)
  blocking collectives  9.66 us (5%)
    unnamed x4, other arithmetic  22.3 us
    dot_general x18, matrix products, convolve(): jnp.einsum('erwc,ck->erwk', window, weight[row_step, col_step], preferred...  20.2 us
    reduce_scatter x1, waiting for transfers between devices, per_device(): lax.psum_scatter(placed.reshape(own_rows * lax.axis_size('tile'), frame_t...  19.8 us
    another operation x50, local copies, waits for them, and re-layouts, per_device(): jnp.stack(columns, axis=-1) * features.shape[3] ** (-0.5)  16 us
    ppermute x3, starting transfers between devices, padded_2(): lax.ppermute(tail, axis, [(i, (i + 1) % count) for i in range(ends)])  15.7 us
    all_to_all x1, waiting for transfers between devices, per_device(): lax.all_to_all(asked, 'edge', split_axis=0, concat_axis=0, tiled=True)  15.4 us
    all_to_all x1, blocking collectives, per_device(): lax.all_to_all(send_target, 'edge', split_axis=0, concat_axis=0, tiled=True)  9.66 us
    ppermute x3, starting transfers between devices, per_device(): lax.ppermute(pose_diagonal, 'tile', [(dev, dev ^ hop) for dev in range(8)])  7.05 us
  transfers between devices with their start and end apart: 13, of which 9 were waited for; matrix products, arithmetic and copies ran while one was open for 4% of the time, Pallas kernels for 0%

profile of v1, /device:TPU:0, one launch (start us, length us, event | category | flops | bytes accessed | tf_op | source)
XLA Modules:
  0.0 204.7 jit_solution(2829787406782188017)
XLA Ops:
  7.2 0.8 fusion.173
  10.2 0.7 select_reduce_fusion
  11.0 9.7 %all_to_all.28 = s32[4,1,4]{2,1,0:T(1,128)S(1)} all-to-all(s32[4,1,4]{2,1,0:T(1,128)S(1)} %bitcast.304), channel_id=1, replica_groups=mesh['edge'=4,'tile'=8] {'edge'}, dimensions={0} | all-to-all | bytes 128 | tf_op jit(solution)/shard_map/all_to_all | solution.py:85
  22.0 1.9 gather_fusion.1
  23.9 2.8 %broadcast_select_fusion = bf16[4,4,6,64,128]{4,3,2,1,0:T(8,128)(2,1)} fusion(bf16[4,4,6,64,128]{4,3,2,1,0:T(8,128)(2,1)} %bitcast.251, pred[4,4]{1,0:T(4,128)(4,1)S(1)} %compare_and_fusion), kind=kLoop, calls=%fused_computation.176 | loop fusion | flops 786432 | bytes 3145744 | tf_op jit(solution)/shard_map/jit(_take)/select_n | solution.py:88
  26.6 4.3 %all-to-all-start.1 = ((bf16[4,4,6,64,128]{4,3,2,1,0:T(8,128)(2,1)}), bf16[4,4,6,64,128]{4,3,2,1,0:T(8,128)(2,1)}, u32[]{:S(2)}, u32[]{:S(2)}) async-start(bf16[4,4,6,64,128]{4,3,2,1,0:T(8,128)(2,1)} %broadcast_select_fusion), calls=%async_computation.1 | async-start | bytes 3145728 | tf_op jit(solution)/shard_map/all_to_all | solution.py:91
  31.0 0.7 gather_fusion
  33.7 15.4 %all-to-all-done.1 = bf16[4,4,6,64,128]{4,3,2,1,0:T(8,128)(2,1)} async-done(((bf16[4,4,6,64,128]{4,3,2,1,0:T(8,128)(2,1)}), bf16[4,4,6,64,128]{4,3,2,1,0:T(8,128)(2,1)}, u32[]{:S(2)}, u32[]{:S(2)}) %all-to-all-start.1) | async-done | bytes 1572896 | tf_op jit(solution)/shard_map/all_to_all | solution.py:91
  49.1 3.2 %all-to-all-start.2 = ((s32[4,1,4]{2,1,0:T(1,128)}), s32[4,1,4]{2,1,0:T(1,128)S(1)}, u32[]{:S(2)}, u32[]{:S(2)}) async-start(s32[4,1,4]{2,1,0:T(1,128)} %bitcast.116), calls=%async_computation.2 | async-start | bytes 4096 | tf_op jit(solution)/shard_map/all_to_all | solution.py:86
  52.4 2.1 %gather_fusion.2 = bf16[8,6,64,128]{3,2,1,0:T(8,128)(2,1)S(1)} fusion(bf16[16,6,64,128]{3,2,1,0:T(8,128)(2,1)} %bitcast.9, s32[1024]{0:T(1024)S(1)} %pad_clamp_fusion), kind=kCustom, calls=%fused_computation.2 | custom fusion | bytes 1572896 | tf_op jit(solution)/shard_map/jit(_take)/gather | solution.py:92
  54.7 1.3 collective-permute-start
  56.0 1.3 collective-permute-start.1
  59.3 2.1 %collective-permute-done.1 = bf16[8,3,64,128]{3,2,1,0:T(8,128)(2,1)S(1)} collective-permute-done((bf16[8,3,64,128]{3,2,1,0:T(8,128)(2,1)S(1)}, bf16[8,3,64,128]{3,2,1,0:T(8,128)(2,1)S(1)}, u32[]{:S(2)}, u32[]{:S(2)}) %collective-permute-start.1) | collective-permute-done | bytes 393248 | tf_op jit(solution)/shard_map/ppermute | solution.py:21
  61.4 1.0 fusion.29
  62.4 7.7 %fusion.75 = (f32[8,6,64]{2,1,0:T(8,128)S(1)}, f32[8,6,64]{2,1,0:T(8,128)S(1)}, f32[8,6,64]{2,1,0:T(8,128)S(1)}, f32[8,6,64]{2,1,0:T(8,128)S(1)}, f32[8,6,64]{2,...) fusion(bf16[8,12,70,128]{3,2,1,0:T(8,128)(2,1)S(1)} %fusion.29,, ...), kind=kLoop, calls=%fused_computation.154 | loop fusion | flops 20788224 | bytes 14364680
  70.1 7.6 %fusion.95 = (f32[8,6,64]{2,1,0:T(8,128)S(1)}, f32[8,6,64]{2,1,0:T(8,128)S(1)}, f32[8,6,64]{2,1,0:T(8,128)S(1)}, f32[8,6,64]{2,1,0:T(8,128)S(1)}, f32[8,6,64]{2,...) fusion(bf16[8,12,70,128]{3,2,1,0:T(8,128)(2,1)S(1)} %fusion.29,, ...), kind=kLoop, calls=%fused_computation.174 | loop fusion | flops 20788224 | bytes 14364680
  77.8 3.6 %fusion.55 = (f32[8,6,64]{2,1,0:T(8,128)S(1)}, f32[8,6,64]{2,1,0:T(8,128)S(1)}, f32[8,6,64]{2,1,0:T(8,128)S(1)}, f32[8,6,64]{2,1,0:T(8,128)S(1)}, f32[8,6,64]{2,...) fusion(bf16[8,12,70,128]{3,2,1,0:T(8,128)(2,1)S(1)} %fusion.29, ...), kind=kLoop, calls=%fused_computation.134 | loop fusion | flops 10199040 | bytes 7176200
  89.4 3.4 %fusion.92 = (f32[8,6,64]{2,1,0:T(8,128)S(1)}, f32[8,6,64]{2,1,0:T(8,128)S(1)}, f32[8,6,64]{2,1,0:T(8,128)S(1)}, f32[8,6,64]{2,1,0:T(8,128)S(1)}, f32[8,6,64]{2,...) fusion(bf16[8,3,64,128]{3,2,1,0:T(8,128)(2,1)S(1)} %collective-permute-done.1, ...), kind=kLoop, calls=%fused_computation.171 | loop fusion | flops 11381760 | bytes 2445320
  93.0 8.1 %stack.199 = f32[8,6,64,49]{2,3,1,0:T(8,128)} concatenate(f32[8,6,64,1]{2,3,1,0:T(1,128)} %copy.199, f32[8,6,64,1]{2,3,1,0:T(1,128)} %copy.200, f32[8,6,64,1]{2,3,1,0:T(1,128)} %copy.201, f32[8,6,64,1]{2,3,1,0:T(1,128)S(1)} %copy.202, f32[8,6,64,1]{2,3,1,0:T(1,128)} %copy.203, f32[8,6,64,1]{2,3,1,0:T(1,128)} %copy.204, f32[8,6,64,1]{2,3,1,0:T(1,128)} %copy.205, ...), dimensions={3} | concatenate | bytes 1204224 | tf_op jit(solution)/shard_map/stack | solution.py:108
  101.1 1.8 maximum_convert_fusion
  103.1 8.0 %collective-permute-start.2 = (bf16[8,1,64,256]{3,2,1,0:T(8,128)(2,1)S(1)}, bf16[8,1,64,256]{3,2,1,0:T(8,128)(2,1)S(1)}, u32[]{:S(2)}, u32[]{:S(2)}) collective-permute-start(bf16[8,1,64,256]{3,2,1,0:T(8,128)(2,1)S(1)} %get-tuple-element.63), channel_id=1, source_target_pairs={{0,1},{1,2},{2,3},{3,4},{4,5},{5,6},{6,7},{8,9},{9,10},{10,11},{11... | collective-permute-start | bytes 786440 | tf_op jit(solution)/shard_map/ppermute | solution.py:19
  111.1 1.3 collective-permute-start.3
  113.0 1.5 collective-permute-done.3
  117.8 2.2 %fusion.15 = f32[8,6,64,256]{3,2,1,0:T(8,128)} fusion(bf16[8,6,64,128]{3,2,1,0:T(8,128)(2,1)S(1)} %maximum_convert_fusion, bf16[8,6,64,128]{3,2,1,0:T(8,128)(2,1)S(1)} %copy-done.2, bf16[8,1,64,256]{3,2,1,0:T(8,128)(2,1)S(1)} %collective-permute-done.2, bf16[3,3,256,256]{3,2,1,0:T(8,128)(2,1)S(1)} %copy-done.4), kind=kOutput, calls=%fused_computation.84 | convolution fusion | flops 408158208 | bytes 5111808 | tf_op jit(solution)/shard_map/erwc,ck->erwk/dot_general | solution.py:39
  120.0 2.3 %fusion.9 = f32[8,6,64,256]{3,2,1,0:T(8,128)} fusion(bf16[8,6,64,128]{3,2,1,0:T(8,128)(2,1)S(1)} %maximum_convert_fusion, bf16[8,1,64,256]{3,2,1,0:T(8,128)(2,1)S(1)} %collective-permute-done.3, bf16[8,6,64,128]{3,2,1,0:T(8,128)(2,1)S(1)} %copy-done.2, bf16[3,3,256,256]{3,2,1,0:T(8,128)(2,1)S(1)} %copy-done.4), kind=kOutput, calls=%fused_computation.80 | convolution fusion | flops 408158208 | bytes 5111808 | tf_op jit(solution)/shard_map/erwc,ck->erwk/dot_general | solution.py:39
  122.3 5.2 %add_divide_fusion = f32[8,6,64,256]{3,2,1,0:T(8,128)} fusion(f32[8,6,64,256]{3,2,1,0:T(8,128)} %fusion.9, f32[8,6,64,256]{3,2,1,0:T(8,128)S(1)} %fusion.34, f32[8,6,64,256]{3,2,1,0:T(8,128)S(1)} %fusion.33, f32[8,6,64,256]{3,2,1,0:T(8,128)S(1)} %fusion.45, f32[8,6,64,256]{3,2,1,0:T(8,128)S(1)} %fusion.32, f32[8,6,64,256]{3,2,1,0:T(8,128)S(1)} %fusion.31, ...), kind=kOutput, calls=%fused_computation.55 | convolution fusion | flops 411303936 | bytes 30539776 | tf_op jit(solution)/shard_map/erwc,ck->erwk/dot_general | solution.py:39
  127.5 1.7 fusion.44
  129.3 6.3 %collective-permute-start.4 = (bf16[8,1,64,256]{3,2,1,0:T(8,128)(2,1)S(1)}, bf16[8,1,64,256]{3,2,1,0:T(8,128)(2,1)S(1)}, u32[]{:S(2)}, u32[]{:S(2)}) collective-permute-start(bf16[8,1,64,256]{3,2,1,0:T(8,128)(2,1)S(1)} %get-tuple-element.61), channel_id=1, source_target_pairs={{0,1},{1,2},{2,3},{3,4},{4,5},{5,6},{6,7},{8,9},{9,10},{10,11},{11... | collective-permute-start | bytes 786440 | tf_op jit(solution)/shard_map/ppermute | solution.py:19
  135.6 1.5 collective-permute-start.5
  137.7 1.3 collective-permute-done.5
  143.4 1.3 copy-done.3
  144.7 2.3 %broadcast_select_fusion.3 = (bf16[8,6,64,128]{3,2,1,0:T(8,128)(2,1)}, bf16[8,6,64,128]{3,2,1,0:T(8,128)(2,1)S(1)}) fusion(bf16[8,6,64,128]{3,2,1,0:T(8,128)(2,1)S(1)} %copy-done.2, pred[8]{0:T(512)(128)(4,1)S(1)} %copy-done.15, bf16[3,3,256,128]{3,2,1,0:T(8,128)(2,1)S(1)} %copy-done.5, bf16[8,8,64,256]{3,2,1,0:T(8,128)(2,1)S(1)} %fusion.4, ...), kind=kOutput, calls=%fused_computation.199 | convolution fusion | flops 207224832 | bytes 18678272 | tf_op jit(solution)/shard_map/erwc,ck->erwk/dot_general | solution.py:39
  147.0 0.7 convolution_bitcast_fusion
  148.4 0.7 compare_select_fusion
  150.1 0.9 fusion.166
  151.0 4.2 %all-to-all-start.3 = ((f32[4,4,72]{2,1,0:T(4,128)}), f32[4,4,72]{2,1,0:T(4,128)S(1)}, u32[]{:S(2)}, u32[]{:S(2)}) async-start(f32[4,4,72]{2,1,0:T(4,128)} %bitcast.126), calls=%async_computation.3 | async-start | bytes 16384 | tf_op jit(solution)/shard_map/all_to_all | solution.py:146
  155.5 4.4 %all-to-all-done.3 = f32[4,4,72]{2,1,0:T(4,128)S(1)} async-done(((f32[4,4,72]{2,1,0:T(4,128)}), f32[4,4,72]{2,1,0:T(4,128)S(1)}, u32[]{:S(2)}, u32[]{:S(2)}) %all-to-all-start.3) | async-done | bytes 4640 | tf_op jit(solution)/shard_map/all_to_all | solution.py:146
  160.4 1.1 convolution_convert_fusion
  161.4 1.3 copy.258
  162.7 0.9 convert_element_type.73
  163.9 2.9 %collective-permute-start.6 = (f32[24,36]{1,0:T(8,128)S(1)}, f32[24,36]{1,0:T(8,128)S(1)}, u32[]{:S(2)}, u32[]{:S(2)}) collective-permute-start(f32[24,36]{1,0:T(8,128)S(1)} %fusion.148), channel_id=1, source_target_pairs={{0,1},{1,0},{2,3},{3,2},{4,5},{5,4},{6,7},{7,6},{8,9},{9,8},{10,11... | collective-permute-start | bytes 10376 | tf_op jit(solution)/shard_map/ppermute | solution.py:188
  166.8 0.8 collective-permute-done.6
  167.7 1.6 collective-permute-start.7
  169.2 2.1 %collective-permute-done.7 = f32[24,36]{1,0:T(8,128)S(1)} collective-permute-done((f32[24,36]{1,0:T(8,128)S(1)}, f32[24,36]{1,0:T(8,128)S(1)}, u32[]{:S(2)}, u32[]{:S(2)}) %collective-permute-start.7) | collective-permute-done | bytes 3488 | tf_op jit(solution)/shard_map/ppermute | solution.py:188
  171.4 2.6 %collective-permute-start.8 = (f32[24,36]{1,0:T(8,128)S(1)}, f32[24,36]{1,0:T(8,128)S(1)}, u32[]{:S(2)}, u32[]{:S(2)}) collective-permute-start(f32[24,36]{1,0:T(8,128)S(1)} %add.172), channel_id=1, source_target_pairs={{0,4},{1,5},{2,6},{3,7},{4,0},{5,1},{6,2},{7,3},{8,12},{9,13},{10,... | collective-permute-start | bytes 10376 | tf_op jit(solution)/shard_map/ppermute | solution.py:188
  173.9 2.0 collective-permute-done.8
  176.6 19.8 %reduce-scatter.2.cloned.1.call-done = bf16[72,144]{1,0:T(8,128)(2,1)} async-done(((bf16[576,144]{1,0:T(8,128)(2,1)}), bf16[72,144]{1,0:T(8,128)(2,1)}) %reduce-scatter.2.cloned.1.call-update) | async-done | bytes 20752 | tf_op jit(solution)/shard_map/reduce_scatter | solution.py:180
  196.4 1.4 convert_element_type.74
  (166 shorter events, 27.0 us)
Async XLA Ops:
  7.2 14.8 %copy-start = (bf16[24,6,64,128]{3,2,1,0:T(8,128)(2,1)S(1)}, bf16[24,6,64,128]{3,2,1,0:T(8,128)(2,1)}, u32[]{:S(2)}) copy-start(bf16[24,6,64,128]{3,2,1,0:T(8,128)(2,1)} %param.11) | copy-start | bytes 7077892
  26.6 22.5 %all-to-all-start.1 = ((bf16[4,4,6,64,128]{4,3,2,1,0:T(8,128)(2,1)}), bf16[4,4,6,64,128]{4,3,2,1,0:T(8,128)(2,1)}, u32[]{:S(2)}, u32[]{:S(2)}) async-start(bf16[4,4,6,64,128]{4,3,2,1,0:T(8,128)(2,1)} %broadcast_select_fusion), calls=%async_computation.1 | async-start | bytes 3145728 | tf_op jit(solution)/shard_map/all_to_all | solution.py:91
  31.0 2.7 %copy-start.14 = (s32[8]{0:T(128)S(1)}, s32[8]{0:T(128)}, u32[]{:S(2)}) copy-start(s32[8]{0:T(128)} %param.13) | copy-start | bytes 100
  31.0 2.7 %copy-start.11 = (s32[8,1]{0,1:T(1,128)S(1)}, s32[8,1]{0,1:T(1,128)}, u32[]{:S(2)}) copy-start(s32[8,1]{0,1:T(1,128)} %param.14) | copy-start | bytes 100
  31.0 2.7 %copy-start.17 = (s32[8]{0:T(128)S(1)}, s32[8]{0:T(128)}, u32[]{:S(2)}) copy-start(s32[8]{0:T(128)} %param.15) | copy-start | bytes 100
  49.1 8.8 %all-to-all-start.2 = ((s32[4,1,4]{2,1,0:T(1,128)}), s32[4,1,4]{2,1,0:T(1,128)S(1)}, u32[]{:S(2)}, u32[]{:S(2)}) async-start(s32[4,1,4]{2,1,0:T(1,128)} %bitcast.116), calls=%async_computation.2 | async-start | bytes 4096 | tf_op jit(solution)/shard_map/all_to_all | solution.py:86
  54.7 4.6 %collective-permute-start = (bf16[8,3,64,128]{3,2,1,0:T(8,128)(2,1)S(1)}, bf16[8,3,64,128]{3,2,1,0:T(8,128)(2,1)S(1)}, u32[]{:S(2)}, u32[]{:S(2)}) collective-permute-start(bf16[8,3,64,128]{3,2,1,0:T(8,128)(2,1)S(1)} %get-tuple-element.65), channel_id=1, source_target_pairs={{0,1},{1,2},{2,3},{3,4},{4,5},{5,6},{6,7},{8,9},{9,10},{10,11},{11... | collective-permute-start | bytes 1179656 | tf_op jit(solution)/shard_map/ppermute | solution.py:19
  56.0 5.4 %collective-permute-start.1 = (bf16[8,3,64,128]{3,2,1,0:T(8,128)(2,1)S(1)}, bf16[8,3,64,128]{3,2,1,0:T(8,128)(2,1)S(1)}, u32[]{:S(2)}, u32[]{:S(2)}) collective-permute-start(bf16[8,3,64,128]{3,2,1,0:T(8,128)(2,1)S(1)} %get-tuple-element.66), channel_id=1, source_target_pairs={{1,0},{2,1},{3,2},{4,3},{5,4},{6,5},{7,6},{9,8},{10,9},{11,10},{12... | collective-permute-start | bytes 1179656 | tf_op jit(solution)/shard_map/ppermute | solution.py:21
  88.1 4.9 %copy-start.6 = (f32[8,6,64,1]{2,3,1,0:T(1,128)S(1)}, f32[8,6,64,1]{2,3,1,0:T(1,128)}, u32[]{:S(2)}) copy-start(f32[8,6,64,1]{2,3,1,0:T(1,128)} %copy.227) | copy-start | bytes 36868
  88.1 4.9 %copy-start.7 = (f32[8,6,64,1]{2,3,1,0:T(1,128)S(1)}, f32[8,6,64,1]{2,3,1,0:T(1,128)}, u32[]{:S(2)}) copy-start(f32[8,6,64,1]{2,3,1,0:T(1,128)} %copy.228) | copy-start | bytes 36868
  88.1 4.9 %copy-start.8 = (f32[8,6,64,1]{2,3,1,0:T(1,128)S(1)}, f32[8,6,64,1]{2,3,1,0:T(1,128)}, u32[]{:S(2)}) copy-start(f32[8,6,64,1]{2,3,1,0:T(1,128)} %copy.229) | copy-start | bytes 36868
  92.7 8.4 %copy-start.9 = (bf16[49,128]{1,0:T(8,128)(2,1)S(1)}, bf16[49,128]{1,0:T(8,128)(2,1)}, u32[]{:S(2)}) copy-start(bf16[49,128]{1,0:T(8,128)(2,1)} %param.17) | copy-start | bytes 37636
  101.1 1.8 copy-start.2
  103.0 9.4 %copy-start.4 = (bf16[3,3,256,256]{3,2,1,0:T(8,128)(2,1)S(1)}, bf16[3,3,256,256]{3,2,1,0:T(8,128)(2,1)}, u32[]{:S(2)}) copy-start(bf16[3,3,256,256]{3,2,1,0:T(8,128)(2,1)} %param.18) | copy-start | bytes 3538948
  103.1 9.9 %collective-permute-start.2 = (bf16[8,1,64,256]{3,2,1,0:T(8,128)(2,1)S(1)}, bf16[8,1,64,256]{3,2,1,0:T(8,128)(2,1)S(1)}, u32[]{:S(2)}, u32[]{:S(2)}) collective-permute-start(bf16[8,1,64,256]{3,2,1,0:T(8,128)(2,1)S(1)} %get-tuple-element.63), channel_id=1, source_target_pairs={{0,1},{1,2},{2,3},{3,4},{4,5},{5,6},{6,7},{8,9},{9,10},{10,11},{11... | collective-permute-start | bytes 786440 | tf_op jit(solution)/shard_map/ppermute | solution.py:19
  111.1 3.4 %collective-permute-start.3 = (bf16[8,1,64,256]{3,2,1,0:T(8,128)(2,1)S(1)}, bf16[8,1,64,256]{3,2,1,0:T(8,128)(2,1)S(1)}, u32[]{:S(2)}, u32[]{:S(2)}) collective-permute-start(bf16[8,1,64,256]{3,2,1,0:T(8,128)(2,1)S(1)} %get-tuple-element.64), channel_id=1, source_target_pairs={{1,0},{2,1},{3,2},{4,3},{5,4},{6,5},{7,6},{9,8},{10,9},{11,10},{12... | collective-permute-start | bytes 786440 | tf_op jit(solution)/shard_map/ppermute | solution.py:21
  129.2 7.9 %copy-start.5 = (bf16[3,3,256,128]{3,2,1,0:T(8,128)(2,1)S(1)}, bf16[3,3,256,128]{3,2,1,0:T(8,128)(2,1)}, u32[]{:S(2)}) copy-start(bf16[3,3,256,128]{3,2,1,0:T(8,128)(2,1)} %param.19) | copy-start | bytes 1769476
  129.3 8.4 %collective-permute-start.4 = (bf16[8,1,64,256]{3,2,1,0:T(8,128)(2,1)S(1)}, bf16[8,1,64,256]{3,2,1,0:T(8,128)(2,1)S(1)}, u32[]{:S(2)}, u32[]{:S(2)}) collective-permute-start(bf16[8,1,64,256]{3,2,1,0:T(8,128)(2,1)S(1)} %get-tuple-element.61), channel_id=1, source_target_pairs={{0,1},{1,2},{2,3},{3,4},{4,5},{5,6},{6,7},{8,9},{9,10},{10,11},{11... | collective-permute-start | bytes 786440 | tf_op jit(solution)/shard_map/ppermute | solution.py:19
  135.6 3.4 %collective-permute-start.5 = (bf16[8,1,64,256]{3,2,1,0:T(8,128)(2,1)S(1)}, bf16[8,1,64,256]{3,2,1,0:T(8,128)(2,1)S(1)}, u32[]{:S(2)}, u32[]{:S(2)}) collective-permute-start(bf16[8,1,64,256]{3,2,1,0:T(8,128)(2,1)S(1)} %get-tuple-element.62), channel_id=1, source_target_pairs={{1,0},{2,1},{3,2},{4,3},{5,4},{6,5},{7,6},{9,8},{10,9},{11,10},{12... | collective-permute-start | bytes 786440 | tf_op jit(solution)/shard_map/ppermute | solution.py:21
  142.8 1.9 copy-start.3
  142.8 1.9 copy-start.15
  144.7 2.3 %copy-start.10 = (bf16[128,24]{0,1:T(8,128)(2,1)S(1)}, bf16[128,24]{0,1:T(8,128)(2,1)}, u32[]{:S(2)}) copy-start(bf16[128,24]{0,1:T(8,128)(2,1)} %param.20) | copy-start | bytes 18436
  147.7 0.7 copy-start.19
  147.9 1.4 copy-start.16
  148.4 6.8 %copy-start.12 = (s32[48]{0:T(128)S(1)}, s32[48]{0:T(128)}, u32[]{:S(2)}) copy-start(s32[48]{0:T(128)} %get-tuple-element.59) | copy-start | bytes 580
  151.0 8.9 %all-to-all-start.3 = ((f32[4,4,72]{2,1,0:T(4,128)}), f32[4,4,72]{2,1,0:T(4,128)S(1)}, u32[]{:S(2)}, u32[]{:S(2)}) async-start(f32[4,4,72]{2,1,0:T(4,128)} %bitcast.126), calls=%async_computation.3 | async-start | bytes 16384 | tf_op jit(solution)/shard_map/all_to_all | solution.py:146
  155.2 41.2 %reduce-scatter.2.cloned.1.call-start = ((), (), s32[]{:S(2)}) async-start(), calls=%async_computation.5 | async-start | bytes 331776 | tf_op jit(solution)/shard_map/reduce_scatter | solution.py:180
  160.3 3.5 %copy-start.13 = (s32[48]{0:T(128)S(1)}, s32[48]{0:T(128)}, u32[]{:S(2)}) copy-start(s32[48]{0:T(128)} %get-tuple-element.59) | copy-start | bytes 580
  160.3 37.5 %copy-start.1 = (bf16[24,6,64,128]{3,2,1,0:T(8,128)(2,1)S(1)}, bf16[24,6,64,128]{3,2,1,0:T(8,128)(2,1)}, u32[]{:S(2)}) copy-start(bf16[24,6,64,128]{3,2,1,0:T(8,128)(2,1)} %param.11) | copy-start | bytes 7077892
  160.4 3.4 %copy-start.18 = (f32[48]{0:T(128)S(1)}, f32[48]{0:T(128)}, u32[]{:S(2)}) copy-start(f32[48]{0:T(128)} %get-tuple-element.58) | copy-start | bytes 580
  163.9 3.7 %collective-permute-start.6 = (f32[24,36]{1,0:T(8,128)S(1)}, f32[24,36]{1,0:T(8,128)S(1)}, u32[]{:S(2)}, u32[]{:S(2)}) collective-permute-start(f32[24,36]{1,0:T(8,128)S(1)} %fusion.148), channel_id=1, source_target_pairs={{0,1},{1,0},{2,3},{3,2},{4,5},{5,4},{6,7},{7,6},{8,9},{9,8},{10,11... | collective-permute-start | bytes 10376 | tf_op jit(solution)/shard_map/ppermute | solution.py:188
  167.7 3.7 %collective-permute-start.7 = (f32[24,36]{1,0:T(8,128)S(1)}, f32[24,36]{1,0:T(8,128)S(1)}, u32[]{:S(2)}, u32[]{:S(2)}) collective-permute-start(f32[24,36]{1,0:T(8,128)S(1)} %add.171), channel_id=1, source_target_pairs={{0,2},{1,3},{2,0},{3,1},{4,6},{5,7},{6,4},{7,5},{8,10},{9,11},{10,... | collective-permute-start | bytes 10376 | tf_op jit(solution)/shard_map/ppermute | solution.py:188
  171.4 4.6 %collective-permute-start.8 = (f32[24,36]{1,0:T(8,128)S(1)}, f32[24,36]{1,0:T(8,128)S(1)}, u32[]{:S(2)}, u32[]{:S(2)}) collective-permute-start(f32[24,36]{1,0:T(8,128)S(1)} %add.172), channel_id=1, source_target_pairs={{0,4},{1,5},{2,6},{3,7},{4,0},{5,1},{6,2},{7,3},{8,12},{9,13},{10,... | collective-permute-start | bytes 10376 | tf_op jit(solution)/shard_map/ppermute | solution.py:188
Sparse Core Ops, SparseCore 0:
  163.7 32.6 reduce-scatter.1
